TPU v7x, 256 devices: a whole 4x4x8 slice. The times are simulated.
256 devices in a mesh: dp: 64 (over x, z, core), rep: 4 (over y).
Axes of the slice: x: 4, y: 4, z: 8, core: 2. Of those that a mesh axis runs over, the one named last changes fastest.
Arguments:
- frames_in: bfloat16 [4, 57344, 1536], P('rep', 'dp')
- lengths: int32 [4, 64, 4], P('rep', 'dp'), may hold values from 1 to 893, as said below
- norm_gain: float32 [1536], replicated, may hold values from 0.5 to 1.5
- norm_bias: float32 [1536], replicated, may hold values from -2 to 2
- w_in: bfloat16 [1536, 3072], P(('dp', 'rep')), may hold values from -0.15625 to 0.15625
- kernel: float32 [31, 1536], replicated, may hold values from -1 to 1
- batch_gain: float32 [1536], replicated, may hold values from 0.5 to 1.5
- batch_bias: float32 [1536], replicated, may hold values from -3 to 3
- w_out: bfloat16 [1536, 1536], P(('dp', 'rep')), may hold values from -0.15625 to 0.15625
Outputs:
- frames_out: bfloat16 [4, 57344, 1536], P('rep', 'dp')
Inputs may be any that keep to these rules, and one draw needn't show every extreme that they name: `lengths`: for each rep index, the devices 2k and 2k + 1 of dp hold 1024 frames together, so each rep index holds 512 frames for each of its dp devices; a device holds at most 896 frames, and some device of every rep index holds exactly 896.
All inputs are finite; a program needn't handle non-finite values.
Results may differ from a plain program's by a relative error of at most 0.0038.
Values may be sent and summed in bfloat16 or wider, within the bound.
A program may use at most 128 MiB of HBM per device.

v0:
```python
import jax
import jax.numpy as jnp
from jax import lax
from jax.sharding import PartitionSpec as P

FR_DEV = 512
EPSILON = 1e-05


def layer_norm(frames, norm_gain, norm_bias):
    values = frames.astype(jnp.float32)
    average = jnp.mean(values, axis=-1, keepdims=True)
    centred = values - average
    spread = jnp.mean(centred * centred, axis=-1, keepdims=True)
    return centred * lax.rsqrt(spread + EPSILON) * norm_gain + norm_bias


def depthwise(gated, labels, kernel):
    half_kernel = kernel.shape[0] // 2
    length_rows = gated.shape[0]
    padded = jnp.pad(gated, ((half_kernel, half_kernel), (0, 0)))
    padded_labels = jnp.pad(labels, (half_kernel, half_kernel), constant_values=-1)
    summed = jnp.zeros(gated.shape, jnp.float32)
    for offset in range(kernel.shape[0]):
        shared = padded_labels[offset : offset + length_rows] == labels
        contribution = jnp.where(
            shared[:, None], padded[offset : offset + length_rows].astype(jnp.float32), 0.0
        )
        summed = summed + contribution * kernel[offset]
    return summed


def project_in(normed, weight_rows):
    return jnp.dot(normed, weight_rows, preferred_element_type=jnp.float32)


def project_out(active, weight_rows):
    return jnp.dot(active, weight_rows, preferred_element_type=jnp.float32)


def on_device(
    frames_in, lengths, norm_gain, norm_bias, w_in, kernel, batch_gain, batch_bias, w_out
):
    local_frames = frames_in[0]
    local_lengths = lengths[0, 0]
    capacity = local_frames.shape[0]
    features = local_frames.shape[1]
    total_count = lax.axis_size("dp") * lax.axis_size("rep") * FR_DEV
    grouped = (w_in, w_out)
    grouped = (
        lax.all_gather(w_in, ("dp", "rep"), axis=0, tiled=True),
        lax.all_gather(w_out, ("dp", "rep"), axis=0, tiled=True),
    )
    rows_here = jnp.arange(capacity, dtype=jnp.int32)
    local_load = jnp.sum(local_lengths)
    bounds = jnp.cumsum(local_lengths)
    labels = jnp.sum((rows_here[:, None] >= bounds[None, :]).astype(jnp.int32), axis=1)
    row_weight = (rows_here < local_load).astype(jnp.float32)[:, None]
    normed = layer_norm(local_frames, norm_gain, norm_bias).astype(jnp.bfloat16)
    projected = project_in(normed, grouped[0])
    gated = (projected[:, :features] * jax.nn.sigmoid(projected[:, features:])).astype(jnp.bfloat16)
    convolved = depthwise(gated, labels, kernel)
    average = lax.psum(jnp.sum(convolved * row_weight, axis=0), ("dp", "rep")) / total_count
    centred = convolved - average
    spread = lax.psum(jnp.sum(centred * centred * row_weight, axis=0), ("dp", "rep")) / total_count
    scaled = centred * lax.rsqrt(spread + EPSILON) * batch_gain + batch_bias
    active = jax.nn.silu(scaled).astype(jnp.bfloat16)
    branch = project_out(active, grouped[1])
    mixed = (local_frames.astype(jnp.float32) + branch).astype(jnp.bfloat16)
    result = jnp.where(rows_here[:, None] < local_load, mixed, jnp.zeros_like(mixed))
    return result[None]


def solution(mesh):
    placed = (
        P("rep", "dp", None),
        P("rep", "dp", None),
        P(),
        P(),
        P(("dp", "rep"), None),
        P(),
        P(),
        P(),
        P(("dp", "rep"), None),
    )
    return jax.shard_map(
        on_device, mesh=mesh, in_specs=placed, out_specs=P("rep", "dp", None), check_vma=False
    )
```

profile of v0, /device:TPU:1, one launch (start us, length us, event | category | flops | bytes accessed | tf_op | source)
XLA Modules:
  0.0 487.7 jit_solution(4124133330554323458)
XLA Ops:
  6.5 0.0 all-gather.7.cloned.1.call-start
  6.5 0.7 all-gather.7.cloned.1.call-update
  7.3 0.0 all-gather.5.cloned.1.call-start
  7.3 0.7 all-gather.5.cloned.1.call-update
  8.0 1.3 reduce_sum.54
  9.3 0.8 reduce-window.8
  10.1 0.6 iota_compare_fusion.1
  10.8 0.7 fusion.26
  11.4 0.1 convert_reduce_fusion.1
  11.5 1.5 slice_reduce_fusion.29
  13.0 1.8 slice_reduce_fusion.30
  14.9 0.1 slice_compare_fusion.26
  14.9 2.2 convert_reduce_fusion
  17.2 2.6 fusion.4
  19.8 0.1 slice_compare_fusion.29
  19.9 0.1 slice_compare_fusion.28
  20.0 0.1 slice_compare_fusion.27
  20.1 111.2 %all-gather.7.cloned.1.call-done = bf16[256,6,1536]{2,1,0:T(8,128)(2,1)} async-done(((bf16[1,6,1536]{2,1,0:T(8,128)(2,1)}), bf16[256,6,1536]{2,1,0:T(8,128)(2,1)}) %all-gather.7.cloned.1.call-update) | async-done | bytes 4718608 | tf_op jit(solution)/shard_map/all_gather | solution.py:52
  131.3 8.5 %reshape.87 = bf16[1536,1536]{1,0:T(8,128)(2,1)} reshape(bf16[256,6,1536]{2,1,0:T(8,128)(2,1)} %all-gather.7.cloned.1.call-done) | data formatting | bytes 9437184
  139.8 0.0 copy-start
  139.8 0.0 copy-start.2
  139.8 0.0 copy-start.3
  139.8 113.5 %all-gather.5.cloned.1.call-done = bf16[256,6,3072]{2,1,0:T(8,128)(2,1)} async-done(((bf16[1,6,3072]{2,1,0:T(8,128)(2,1)}), bf16[256,6,3072]{2,1,0:T(8,128)(2,1)}) %all-gather.5.cloned.1.call-update) | async-done | bytes 9437200 | tf_op jit(solution)/shard_map/all_gather | solution.py:51
  253.3 14.2 %reshape.85 = bf16[1536,3072]{1,0:T(8,128)(2,1)} reshape(bf16[256,6,3072]{2,1,0:T(8,128)(2,1)} %all-gather.5.cloned.1.call-done) | data formatting | bytes 18874368
  267.5 0.0 copy-done
  267.5 0.0 copy-done.2
  267.5 0.0 copy-done.3
  267.5 11.3 %fusion.16 = f32[896,3072]{1,0:T(8,128)S(1)} fusion(bf16[1536,3072]{1,0:T(8,128)(2,1)} %reshape.85, bf16[1,896,1536]{2,1,0:T(8,128)(2,1)S(1)} %copy-done, f32[1536]{0:T(1024)S(1)} %copy-done.2, f32[1536]{0:T(1024)S(1)} %copy-done.3, f32[896]{0:T(1024)S(1)} %add_rsqrt_fusion.1, f32[896]{0:T(1024)S(1)} %broadcast_multiply_fusion.1), kind=kOutput, calls=%fused_computation.23 | convolution fusion | flops 8463974400 | bytes 23219200 | tf_op jit(solution)/shard_map/dot_general | solution.py:34
  278.8 1.5 fusion.13
  280.4 0.0 copy-start.4
  280.4 0.0 copy-start.5
  280.4 38.3 %multiply_reduce_fusion.1 = (f32[1536]{0:T(1024)S(1)}, f32[896,1536]{1,0:T(8,128)}) fusion(f32[896]{0:T(1024)S(1)} %fusion.26, f32[1536]{0:T(1024)S(1)} %get-tuple-element.34, pred[896]{0:T(1024)(128)(4,1)S(1)} %get-tuple-element.67, f32[1536]{0:T(1024)S(1)} %get-tuple-element.35, pred[896]{0:T(1024)(128)(4,1)S(1)} %get-tuple-element.39, ...), kind=kLoop, calls=%fused_computation.18 | loop fusion | flops 170654208 | bytes 8484608 | tf_op jit(solution)/shard_map/reduce_sum | solution.py:63
  318.7 0.0 copy-start.1
  318.7 74.8 %psum.14 = f32[1536]{0:T(1024)S(1)} all-reduce(f32[1536]{0:T(1024)S(1)} %get-tuple-element.36), channel_id=1, replica_groups=mesh['dp'=64,'rep'=4] {'dp','rep'}, use_global_device_ids=true, to_apply=%region_6.7 | all-reduce | flops 1536 | bytes 12288 | tf_op jit(solution)/shard_map/psum | solution.py:63
  393.5 3.3 multiply_reduce_fusion
  396.8 73.6 %psum.15 = f32[1536]{0:T(1024)S(1)} all-reduce(f32[1536]{0:T(1024)S(1)} %multiply_reduce_fusion), channel_id=1, replica_groups=mesh['dp'=64,'rep'=4] {'dp','rep'}, use_global_device_ids=true, to_apply=%region_8.9 | all-reduce | flops 1536 | bytes 12288 | tf_op jit(solution)/shard_map/psum | solution.py:65
  470.4 0.0 copy-done.4
  470.4 0.0 copy-done.5
  470.4 0.0 copy-done.1
  470.4 10.4 %fusion.15 = bf16[1,896,1536]{2,1,0:T(8,128)(2,1)} fusion(bf16[1536,1536]{1,0:T(8,128)(2,1)} %reshape.87, bf16[1,896,1536]{2,1,0:T(8,128)(2,1)S(1)} %copy-done.1, f32[896,1536]{1,0:T(8,128)} %get-tuple-element.37, f32[1536]{0:T(1024)S(1)} %copy-done.4, f32[1536]{0:T(1024)S(1)} %copy-done.5, f32[1536]{0:T(1024)S(1)} %add_rsqrt_fusion, ...), kind=kOutput, calls=%fused_computation.22 | convolution fusion | flops 4245749760 | bytes 15754112 | tf_op jit(solution)/shard_map/dot_general | solution.py:38
  (4 shorter events, 0.0 us)
Async XLA Ops:
  6.5 124.8 %all-gather.7.cloned.1.call-start = ((), (), s32[]{:S(2)}) async-start(), calls=%async_computation.1 | async-start | bytes 6316032 | tf_op jit(solution)/shard_map/all_gather | solution.py:52
  7.3 246.1 %all-gather.5.cloned.1.call-start = ((), (), s32[]{:S(2)}) async-start(), calls=%async_computation | async-start | bytes 12632064 | tf_op jit(solution)/shard_map/all_gather | solution.py:51
  139.8 127.7 %copy-start = (bf16[1,896,1536]{2,1,0:T(8,128)(2,1)S(1)}, bf16[1,896,1536]{2,1,0:T(8,128)(2,1)}, u32[]{:S(2)}) copy-start(bf16[1,896,1536]{2,1,0:T(8,128)(2,1)} %param.9) | copy-start | bytes 8257540
  139.8 127.7 %copy-start.2 = (f32[1536]{0:T(1024)S(1)}, f32[1536]{0:T(1024)}, u32[]{:S(2)}) copy-start(f32[1536]{0:T(1024)} %param.12) | copy-start | bytes 18436
  139.8 127.7 %copy-start.3 = (f32[1536]{0:T(1024)S(1)}, f32[1536]{0:T(1024)}, u32[]{:S(2)}) copy-start(f32[1536]{0:T(1024)} %param.11) | copy-start | bytes 18436
  280.4 190.1 %copy-start.4 = (f32[1536]{0:T(1024)S(1)}, f32[1536]{0:T(1024)}, u32[]{:S(2)}) copy-start(f32[1536]{0:T(1024)} %param.16) | copy-start | bytes 18436
  280.4 190.1 %copy-start.5 = (f32[1536]{0:T(1024)S(1)}, f32[1536]{0:T(1024)}, u32[]{:S(2)}) copy-start(f32[1536]{0:T(1024)} %param.15) | copy-start | bytes 18436
  318.7 151.7 %copy-start.1 = (bf16[1,896,1536]{2,1,0:T(8,128)(2,1)S(1)}, bf16[1,896,1536]{2,1,0:T(8,128)(2,1)}, u32[]{:S(2)}) copy-start(bf16[1,896,1536]{2,1,0:T(8,128)(2,1)} %param.9) | copy-start | bytes 8257540
Sparse Core Ops, SparseCore 0:
  11.2 120.0 all-gather.6
  135.1 118.1 all-gather.4
where the time goes:
time: 489 us; the launch traced here: 488 us
  waiting for transfers between devices  226 us (46%)
  blocking collectives  148 us (30%)
  other arithmetic  51.8 us (11%)
  local copies, waits for them, and re-layouts  26 us (5%)
  matrix products  21.8 us (4%)
  between operations  13.5 us (3%)
    all_gather x1, waiting for transfers between devices, on_device(): lax.all_gather(w_in, ('dp', 'rep'), axis=0, tiled=True)  114 us
    all_gather x1, waiting for transfers between devices, on_device(): lax.all_gather(w_out, ('dp', 'rep'), axis=0, tiled=True)  111 us
    psum x1, blocking collectives, on_device(): lax.psum(jnp.sum(convolved * row_weight, axis=0), ('dp', 'rep'))  74.8 us
    psum x1, blocking collectives, on_device(): lax.psum(jnp.sum(centred * centred * row_weight, axis=0), ('dp', 'rep'))  73.6 us
    reduce_sum x1, other arithmetic, on_device(): jnp.sum(convolved * row_weight, axis=0)  38.3 us
    unnamed x14, local copies, waits for them, and re-layouts  22.6 us
    dot_general x1, matrix products, project_in(): return jnp.dot(normed, weight_rows, preferred_element_type=jnp.float32)  11.3 us
    dot_general x1, matrix products, project_out(): return jnp.dot(active, weight_rows, preferred_element_type=jnp.float32)  10.4 us
  transfers between devices with their start and end apart: 2, of which 2 were waited for; matrix products, arithmetic and copies ran while one was open for 4% of the time, Pallas kernels for 0%

commit v1 on v0

--- a/solution.py
+++ b/solution.py
@@ -62,7 +62,10 @@
     convolved = depthwise(gated, labels, kernel)
     average = lax.psum(jnp.sum(convolved * row_weight, axis=0), ("dp", "rep")) / total_count
     centred = convolved - average
-    spread = lax.psum(jnp.sum(centred * centred * row_weight, axis=0), ("dp", "rep")) / total_count
+    spread = (
+        lax.psum(lax.psum(jnp.sum(centred * centred * row_weight, axis=0), "dp"), "rep")
+        / total_count
+    )
     scaled = centred * lax.rsqrt(spread + EPSILON) * batch_gain + batch_bias
     active = jax.nn.silu(scaled).astype(jnp.bfloat16)
     branch = project_out(active, grouped[1])

time: 489 us -> 551 us (1.13)
  blocking collectives: 148 us -> 209 us
    psum x1 -> x2, blocking collectives: 73.6 us -> 135 us  [the longest x1 126 us: on_device(): lax.psum(jnp.sum(centred * centred * row_weight, axis=0), 'dp')]
where the time goes in v1:
time: 551 us; the launch traced here: 549 us
  waiting for transfers between devices  226 us (41%)
  blocking collectives  209 us (38%)
  other arithmetic  51.8 us (9%)
  local copies, waits for them, and re-layouts  26 us (5%)
  matrix products  21.8 us (4%)
  between operations  13.5 us (2%)
    psum x1, blocking collectives, on_device(): lax.psum(jnp.sum(centred * centred * row_weight, axis=0), 'dp')  126 us
    all_gather x1, waiting for transfers between devices, on_device(): lax.all_gather(w_in, ('dp', 'rep'), axis=0, tiled=True)  114 us
    all_gather x1, waiting for transfers between devices, on_device(): lax.all_gather(w_out, ('dp', 'rep'), axis=0, tiled=True)  111 us
    psum x1, blocking collectives, on_device(): lax.psum(jnp.sum(convolved * row_weight, axis=0), ('dp', 'rep'))  74.8 us
    reduce_sum x1, other arithmetic, on_device(): jnp.sum(convolved * row_weight, axis=0)  38.3 us
    unnamed x14, local copies, waits for them, and re-layouts  22.6 us
    dot_general x1, matrix products, project_in(): return jnp.dot(normed, weight_rows, preferred_element_type=jnp.float32)  11.3 us
  transfers between devices with their start and end apart: 2, of which 2 were waited for; matrix products, arithmetic and copies ran while one was open for 4% of the time, Pallas kernels for 0%

profile of v1, /device:TPU:1, one launch (start us, length us, event | category | flops | bytes accessed | tf_op | source)
XLA Modules:
  0.0 548.6 jit_solution(4188371844213610456)
XLA Ops:
  6.5 0.0 all-gather.7.cloned.1.call-start
  6.5 0.7 all-gather.7.cloned.1.call-update
  7.3 0.0 all-gather.5.cloned.1.call-start
  7.3 0.7 all-gather.5.cloned.1.call-update
  8.0 1.3 reduce_sum.54
  9.3 0.8 reduce-window.8
  10.1 0.6 iota_compare_fusion.1
  10.8 0.7 fusion.26
  11.4 0.1 convert_reduce_fusion.1
  11.5 1.5 slice_reduce_fusion.29
  13.0 1.8 slice_reduce_fusion.30
  14.9 0.1 slice_compare_fusion.26
  14.9 2.2 convert_reduce_fusion
  17.2 2.6 fusion.4
  19.8 0.1 slice_compare_fusion.29
  19.9 0.1 slice_compare_fusion.28
  20.0 0.1 slice_compare_fusion.27
  20.1 111.2 %all-gather.7.cloned.1.call-done = bf16[256,6,1536]{2,1,0:T(8,128)(2,1)} async-done(((bf16[1,6,1536]{2,1,0:T(8,128)(2,1)}), bf16[256,6,1536]{2,1,0:T(8,128)(2,1)}) %all-gather.7.cloned.1.call-update) | async-done | bytes 4718608 | tf_op jit(solution)/shard_map/all_gather | solution.py:52
  131.3 8.5 %reshape.87 = bf16[1536,1536]{1,0:T(8,128)(2,1)} reshape(bf16[256,6,1536]{2,1,0:T(8,128)(2,1)} %all-gather.7.cloned.1.call-done) | data formatting | bytes 9437184
  139.8 0.0 copy-start
  139.8 0.0 copy-start.2
  139.8 0.0 copy-start.3
  139.8 113.5 %all-gather.5.cloned.1.call-done = bf16[256,6,3072]{2,1,0:T(8,128)(2,1)} async-done(((bf16[1,6,3072]{2,1,0:T(8,128)(2,1)}), bf16[256,6,3072]{2,1,0:T(8,128)(2,1)}) %all-gather.5.cloned.1.call-update) | async-done | bytes 9437200 | tf_op jit(solution)/shard_map/all_gather | solution.py:51
  253.3 14.2 %reshape.85 = bf16[1536,3072]{1,0:T(8,128)(2,1)} reshape(bf16[256,6,3072]{2,1,0:T(8,128)(2,1)} %all-gather.5.cloned.1.call-done) | data formatting | bytes 18874368
  267.5 0.0 copy-done
  267.5 0.0 copy-done.2
  267.5 0.0 copy-done.3
  267.5 11.3 %fusion.16 = f32[896,3072]{1,0:T(8,128)S(1)} fusion(bf16[1536,3072]{1,0:T(8,128)(2,1)} %reshape.85, bf16[1,896,1536]{2,1,0:T(8,128)(2,1)S(1)} %copy-done, f32[1536]{0:T(1024)S(1)} %copy-done.2, f32[1536]{0:T(1024)S(1)} %copy-done.3, f32[896]{0:T(1024)S(1)} %add_rsqrt_fusion.1, f32[896]{0:T(1024)S(1)} %broadcast_multiply_fusion.1), kind=kOutput, calls=%fused_computation.23 | convolution fusion | flops 8463974400 | bytes 23219200 | tf_op jit(solution)/shard_map/dot_general | solution.py:34
  278.8 1.5 fusion.13
  280.4 0.0 copy-start.4
  280.4 0.0 copy-start.5
  280.4 38.3 %multiply_reduce_fusion.1 = (f32[1536]{0:T(1024)S(1)}, f32[896,1536]{1,0:T(8,128)}) fusion(f32[896]{0:T(1024)S(1)} %fusion.26, f32[1536]{0:T(1024)S(1)} %get-tuple-element.34, pred[896]{0:T(1024)(128)(4,1)S(1)} %get-tuple-element.67, f32[1536]{0:T(1024)S(1)} %get-tuple-element.35, pred[896]{0:T(1024)(128)(4,1)S(1)} %get-tuple-element.39, ...), kind=kLoop, calls=%fused_computation.18 | loop fusion | flops 170654208 | bytes 8484608 | tf_op jit(solution)/shard_map/reduce_sum | solution.py:63
  318.7 0.0 copy-start.1
  318.7 74.8 %psum.21 = f32[1536]{0:T(1024)S(1)} all-reduce(f32[1536]{0:T(1024)S(1)} %get-tuple-element.36), channel_id=1, replica_groups=mesh['dp'=64,'rep'=4] {'dp','rep'}, use_global_device_ids=true, to_apply=%region_6.7 | all-reduce | flops 1536 | bytes 12288 | tf_op jit(solution)/shard_map/psum | solution.py:63
  393.5 3.3 multiply_reduce_fusion
  396.8 126.1 %psum.22 = f32[1536]{0:T(1024)S(1)} all-reduce(f32[1536]{0:T(1024)S(1)} %multiply_reduce_fusion), channel_id=1, replica_groups=mesh['dp'=64,'rep'=4] {'dp'}, use_global_device_ids=true, to_apply=%region_8.9 | all-reduce | flops 1536 | bytes 12288 | tf_op jit(solution)/shard_map/psum | solution.py:66
  522.9 8.4 %psum.23 = f32[1536]{0:T(1024)S(1)} all-reduce(f32[1536]{0:T(1024)S(1)} %psum.22), channel_id=1, replica_groups=mesh['dp'=64,'rep'=4] {'rep'}, use_global_device_ids=true, to_apply=%region_9.10 | all-reduce | flops 1536 | bytes 12288 | tf_op jit(solution)/shard_map/psum | solution.py:66
  531.3 0.0 copy-done.4
  531.3 0.0 copy-done.5
  531.4 0.0 copy-done.1
  531.4 10.4 %fusion.15 = bf16[1,896,1536]{2,1,0:T(8,128)(2,1)} fusion(bf16[1536,1536]{1,0:T(8,128)(2,1)} %reshape.87, bf16[1,896,1536]{2,1,0:T(8,128)(2,1)S(1)} %copy-done.1, f32[896,1536]{1,0:T(8,128)} %get-tuple-element.37, f32[1536]{0:T(1024)S(1)} %copy-done.4, f32[1536]{0:T(1024)S(1)} %copy-done.5, f32[1536]{0:T(1024)S(1)} %add_rsqrt_fusion, ...), kind=kOutput, calls=%fused_computation.22 | convolution fusion | flops 4245749760 | bytes 15754112 | tf_op jit(solution)/shard_map/dot_general | solution.py:38
  (4 shorter events, 0.0 us)
Async XLA Ops:
  6.5 124.8 %all-gather.7.cloned.1.call-start = ((), (), s32[]{:S(2)}) async-start(), calls=%async_computation.1 | async-start | bytes 6316032 | tf_op jit(solution)/shard_map/all_gather | solution.py:52
  7.3 246.1 %all-gather.5.cloned.1.call-start = ((), (), s32[]{:S(2)}) async-start(), calls=%async_computation | async-start | bytes 12632064 | tf_op jit(solution)/shard_map/all_gather | solution.py:51
  139.8 127.7 %copy-start = (bf16[1,896,1536]{2,1,0:T(8,128)(2,1)S(1)}, bf16[1,896,1536]{2,1,0:T(8,128)(2,1)}, u32[]{:S(2)}) copy-start(bf16[1,896,1536]{2,1,0:T(8,128)(2,1)} %param.9) | copy-start | bytes 8257540
  139.8 127.7 %copy-start.2 = (f32[1536]{0:T(1024)S(1)}, f32[1536]{0:T(1024)}, u32[]{:S(2)}) copy-start(f32[1536]{0:T(1024)} %param.12) | copy-start | bytes 18436
  139.8 127.7 %copy-start.3 = (f32[1536]{0:T(1024)S(1)}, f32[1536]{0:T(1024)}, u32[]{:S(2)}) copy-start(f32[1536]{0:T(1024)} %param.11) | copy-start | bytes 18436
  280.4 251.0 %copy-start.4 = (f32[1536]{0:T(1024)S(1)}, f32[1536]{0:T(1024)}, u32[]{:S(2)}) copy-start(f32[1536]{0:T(1024)} %param.16) | copy-start | bytes 18436
  280.4 251.0 %copy-start.5 = (f32[1536]{0:T(1024)S(1)}, f32[1536]{0:T(1024)}, u32[]{:S(2)}) copy-start(f32[1536]{0:T(1024)} %param.15) | copy-start | bytes 18436
  318.7 212.6 %copy-start.1 = (bf16[1,896,1536]{2,1,0:T(8,128)(2,1)S(1)}, bf16[1,896,1536]{2,1,0:T(8,128)(2,1)}, u32[]{:S(2)}) copy-start(bf16[1,896,1536]{2,1,0:T(8,128)(2,1)} %param.9) | copy-start | bytes 8257540
Sparse Core Ops, SparseCore 0:
  11.2 120.0 all-gather.6
  135.1 118.1 all-gather.4
